TPU v7x, 32 devices: a whole 2x2x4 slice. The times are simulated.
32 devices in a mesh: group: 2 (over x), expert: 16 (over z, y, core).
Axes of the slice: x: 2, y: 2, z: 4, core: 2. Of those that a mesh axis runs over, the one named last changes fastest.
Arguments:
- tokens: bfloat16 [64, 256, 1024], P(('group', 'expert')), parts along dimension 0, may hold values from -6 to 6
- w_qkv: bfloat16 [1024, 3072], P('expert'), may hold values from -0.1875 to 0.1875
- w_attn_out: bfloat16 [1024, 1024], P('expert'), may hold values from -0.1875 to 0.1875
- slot_keys: bfloat16 [1024, 32], replicated, may hold values from -0.5 to 0.5
- w_expert_in: bfloat16 [16, 1024, 2048], P('expert'), may hold values from -0.375 to 0.375
- w_expert_out: bfloat16 [16, 2048, 1024], P('expert'), may hold values from -0.125 to 0.125
Outputs:
- block_out: bfloat16 [64, 256, 1024], P(('group', 'expert')), parts along dimension 0
There are 2 independent parts, one for each index of `group`. A program takes and returns all parts, laid end to end along the dimension named above; an argument that names none is the same for every part. Nothing has to cross between parts.
All inputs are finite; a program needn't handle non-finite values.
Results may differ from a plain program's by a relative error of at most 0.009.
Values may be sent and summed in bfloat16 or wider, within the bound.
No kernel may reach another device: no remote copies, remote signals or barrier semaphores. Data moves between devices by JAX's collectives and lax.ppermute only.
A program may use at most 64 MiB of HBM per device.

v0:
```python
import math
import jax
import jax.numpy as jnp
from jax import lax
from jax.sharding import PartitionSpec as P

HEADS = 16


def layer_norm(values):
    center = values - jnp.mean(values, axis=-1, keepdims=True)
    spread = jnp.mean(center * center, axis=-1, keepdims=True)
    return center * lax.rsqrt(spread + 1e-06)


def on_device(tokens, w_qkv, w_attn_out, slot_keys, w_expert_in, w_expert_out):
    image_count, length, model_width = tokens.shape
    head_count = HEADS
    head_width = model_width // head_count
    row_count = image_count * length
    normed = (
        layer_norm(tokens.astype(jnp.float32)).astype(jnp.bfloat16).reshape(row_count, model_width)
    )
    full_qkv = lax.all_gather(w_qkv, "expert", axis=0, tiled=True)
    qkv = jnp.dot(normed, full_qkv, preferred_element_type=jnp.float32)
    packed = qkv.astype(jnp.bfloat16).reshape(image_count, length, 3, head_count, head_width)
    query = packed[:, :, 0]
    keys = packed[:, :, 1]
    values = packed[:, :, 2]
    scores = jnp.einsum(
        "bqhd,bkhd->bhqk", query, keys, preferred_element_type=jnp.float32
    ) / math.sqrt(head_width)
    weights = jax.nn.softmax(scores, axis=-1).astype(jnp.bfloat16)
    attended = jnp.einsum(
        "bhqk,bkhd->bqhd", weights, values, preferred_element_type=jnp.float32
    ).astype(jnp.bfloat16)
    attended = attended.reshape(row_count, model_width)
    full_out = lax.all_gather(w_attn_out, "expert", axis=0, tiled=True)
    projected = jnp.dot(attended, full_out, preferred_element_type=jnp.float32)
    resid = tokens.astype(jnp.float32) + projected.reshape(image_count, length, model_width)
    normed_two = layer_norm(resid).astype(jnp.bfloat16)
    slot_count = slot_keys.shape[1]
    logits = jnp.dot(
        normed_two.reshape(row_count, model_width), slot_keys, preferred_element_type=jnp.float32
    )
    logits = logits.reshape(image_count, length, slot_count)
    dispatch = jax.nn.softmax(logits, axis=1).astype(jnp.bfloat16)
    combine = jax.nn.softmax(logits, axis=2).astype(jnp.bfloat16)
    slot_inputs = jnp.einsum(
        "bsn,bsd->bnd", dispatch, normed_two, preferred_element_type=jnp.float32
    ).astype(jnp.bfloat16)
    sources = lax.axis_size("expert")
    expert_here = w_expert_in.shape[0]
    pairs = slot_count // (sources * expert_here)
    block = lax.all_to_all(slot_inputs, "expert", split_axis=1, concat_axis=1, tiled=True)
    batch = block.shape[0]
    arranged = block.reshape(batch, sources, expert_here, pairs, model_width)
    hidden = jnp.einsum(
        "bnepd,edh->bneph", arranged, w_expert_in, preferred_element_type=jnp.float32
    )
    hidden = jax.nn.gelu(hidden, approximate=False).astype(jnp.bfloat16)
    answer = jnp.einsum(
        "bneph,ehd->bnepd", hidden, w_expert_out, preferred_element_type=jnp.float32
    )
    answered = answer.astype(jnp.bfloat16).reshape(batch, slot_count, model_width)
    slot_outputs = lax.all_to_all(answered, "expert", split_axis=1, concat_axis=1, tiled=True)
    mixed = jnp.einsum("bsn,bnd->bsd", combine, slot_outputs, preferred_element_type=jnp.float32)
    return (resid + mixed).astype(jnp.bfloat16)


def solution(mesh):
    placed = (
        P(("group", "expert"), None, None),
        P("expert", None),
        P("expert", None),
        P(),
        P("expert", None, None),
        P("expert", None, None),
    )
    return jax.shard_map(
        on_device,
        mesh=mesh,
        in_specs=placed,
        out_specs=P(("group", "expert"), None, None),
        check_vma=False,
    )
```

profile of v0, /device:TPU:0, one launch (start us, length us, event | category | flops | bytes accessed | tf_op | source)
XLA Modules:
  0.0 159.9 jit_solution(4813306679087702941)
XLA Ops:
  6.5 0.0 copy-start
  6.5 0.0 all-gather.3.cloned.1.call-start
  6.5 0.7 all-gather.3.cloned.1.call-update
  7.3 0.0 all-gather.5.cloned.1.call-start
  7.3 0.7 all-gather.5.cloned.1.call-update
  8.0 1.4 convert_reduce_fusion
  9.5 0.0 copy-done.1
  9.5 0.4 fusion.14
  9.9 0.3 fusion.15
  10.2 64.0 %all-gather.3.cloned.1.call-done = bf16[1024,3072]{1,0:T(8,128)(2,1)} async-done(((bf16[64,3072]{1,0:T(8,128)(2,1)}), bf16[1024,3072]{1,0:T(8,128)(2,1)}) %all-gather.3.cloned.1.call-update) | async-done | bytes 6291472 | tf_op jit(solution)/shard_map/all_gather | solution.py:24
  74.2 7.5 %convolution_convert_fusion = bf16[512,3072]{1,0:T(8,128)(2,1)} fusion(bf16[512,1024]{1,0:T(8,128)(2,1)S(1)} %bitcast.133, bf16[1024,3072]{1,0:T(8,128)(2,1)} %all-gather.3.cloned.1.call-done), kind=kOutput, calls=%fused_computation.7 | convolution fusion | flops 3222798336 | bytes 10485760 | tf_op jit(solution)/shard_map/dot_general | solution.py:25
  81.8 8.6 %reshape.80 = bf16[2,256,3,16,64]{4,3,2,1,0:T(8,128)(2,1)} reshape(bf16[512,3072]{1,0:T(8,128)(2,1)} %convolution_convert_fusion) | data formatting | bytes 6291456 | tf_op jit(solution)/shard_map/reshape | solution.py:26
  90.4 6.0 %fusion.110 = (bf16[2,256,1,16,64]{4,3,2,1,0:T(8,128)(2,1)S(1)}, bf16[2,256,1,16,64]{4,3,2,1,0:T(8,128)(2,1)}, bf16[2,256,1,16,64]{4,3,2,1,0:T(8,128)(2,1)}) fusion(bf16[2,256,3,16,64]{4,3,2,1,0:T(8,128)(2,1)} %reshape.80), kind=kLoop, calls=%fused_computation.118 | loop fusion | bytes 6291456 | tf_op jit(solution)/shard_map/slice | solution.py:29
  96.4 3.6 %copy.48 = bf16[2,256,1,16,64]{1,4,3,0,2:T(8,128)(2,1)} copy(bf16[2,256,1,16,64]{4,3,2,1,0:T(8,128)(2,1)} %get-tuple-element.6) | data formatting | bytes 2097152
  99.9 3.5 %copy.49 = bf16[2,256,1,16,64]{1,4,3,0,2:T(8,128)(2,1)} copy(bf16[2,256,1,16,64]{4,3,2,1,0:T(8,128)(2,1)} %get-tuple-element.7) | data formatting | bytes 2097152
  103.5 2.5 %copy.47 = bf16[2,256,1,16,64]{1,4,3,0,2:T(8,128)(2,1)} copy(bf16[2,256,1,16,64]{4,3,2,1,0:T(8,128)(2,1)S(1)} %get-tuple-element.5) | data formatting | bytes 2097152
  106.0 2.8 %fusion.31 = f32[2,16,256,256]{2,3,1,0:T(8,128)S(1)} fusion(bf16[2,256,1,16,64]{1,4,3,0,2:T(8,128)(2,1)} %copy.49, bf16[2,256,1,16,64]{1,4,3,0,2:T(8,128)(2,1)} %copy.48), kind=kOutput, calls=%fused_computation.34 | convolution fusion | flops 268435456 | bytes 10485760 | tf_op jit(solution)/shard_map/bqhd,bkhd->bhqk/dot_general | solution.py:30
  108.8 0.0 copy-start.2
  108.8 6.3 %fusion.111 = (f32[2,16,256]{2,1,0:T(8,128)S(1)}, f32[2,16,256,256]{2,3,1,0:T(8,128)S(1)}) fusion(f32[2,16,256,256]{2,3,1,0:T(8,128)S(1)} %fusion.31), kind=kOutput, calls=%fused_computation.119 | output fusion | flops 8388863 | bytes 16809984 | tf_op jit(solution)/shard_map/sub | solution.py:33
  115.1 1.8 %fusion.20 = bf16[2,16,64,256]{3,2,1,0:T(8,128)(2,1)} fusion(f32[2,16,256,256]{2,3,1,0:T(8,128)S(1)} %get-tuple-element.9, f32[2,16,256]{2,1,0:T(8,128)S(1)} %get-tuple-element.8, bf16[2,256,1,16,64]{1,4,3,0,2:T(8,128)(2,1)S(1)} %copy-done.2), kind=kOutput, calls=%fused_computation.26 | convolution fusion | flops 273154048 | bytes 10518528 | tf_op jit(solution)/shard_map/bhqk,bkhd->bqhd/dot_general | solution.py:34
  117.0 3.3 %fusion.112 = (f32[2,256]{1,0:T(2,128)S(1)}, f32[2,256,1024]{2,1,0:T(8,128)S(1)}) fusion(bf16[2,256,1024]{1,2,0:T(8,128)(2,1)} %bitcast.134, bf16[1024,1024]{1,0:T(8,128)(2,1)} %all-gather.5.cloned.1.call-done, bf16[2,256,1024]{2,1,0:T(8,128)(2,1)S(1)} %copy-done.1), kind=kOutput, calls=%fused_computation.120 | convolution fusion | flops 1075314176 | bytes 6293504 | tf_op jit(solution)/shard_map/dot_general | solution.py:39
  120.2 0.4 multiply_reduce_fusion.1
  120.6 0.5 fusion.54
  121.2 0.2 fusion.113
  121.3 0.5 convolution_convert_fusion.1
  121.8 0.1 copy.37
  122.0 11.3 %all_to_all.10 = bf16[2,32,1024]{2,0,1:T(2,128)(2,1)S(1)} all-to-all(bf16[2,32,1024]{2,0,1:T(2,128)(2,1)S(1)} %copy.37), channel_id=1, replica_groups=mesh['group'=2,'expert'=16] {'expert'}, dimensions={1} | all-to-all | bytes 262144 | tf_op jit(solution)/shard_map/all_to_all | solution.py:55
  133.2 6.1 %fusion.24 = bf16[2,16,1,2,1024]{4,1,3,0,2:T(8,128)(2,1)S(1)} fusion(bf16[1,2048,1024]{2,1,0:T(8,128)(2,1)} %param.11, bf16[1,1024,2048]{2,1,0:T(8,128)(2,1)} %param.10, bf16[2,16,2,1024]{3,0,2,1:T(2,128)(2,1)S(1)} %bitcast.135), kind=kOutput, calls=%fused_computation.29 | convolution fusion | flops 545456128 | bytes 8650752 | tf_op jit(solution)/shard_map/bneph,ehd->bnepd/dot_general | solution.py:62
  139.3 0.8 copy.39
  140.1 3.5 %all-to-all-start.1 = ((bf16[2,32,1024]{2,0,1:T(2,128)(2,1)}), bf16[2,32,1024]{2,0,1:T(2,128)(2,1)S(1)}, u32[]{:S(2)}, u32[]{:S(2)}) async-start(bf16[2,32,1024]{2,0,1:T(2,128)(2,1)} %bitcast.27), calls=%async_computation.1 | async-start | bytes 262144 | tf_op jit(solution)/shard_map/all_to_all | solution.py:66
  143.7 7.9 %all-to-all-done.1 = bf16[2,32,1024]{2,0,1:T(2,128)(2,1)S(1)} async-done(((bf16[2,32,1024]{2,0,1:T(2,128)(2,1)}), bf16[2,32,1024]{2,0,1:T(2,128)(2,1)S(1)}, u32[]{:S(2)}, u32[]{:S(2)}) %all-to-all-start.1) | async-done | bytes 131104 | tf_op jit(solution)/shard_map/all_to_all | solution.py:66
  151.6 1.5 add_convert_fusion
  (9 shorter events, 0.1 us)
Async XLA Ops:
  6.5 114.1 %copy-start = (bf16[1024,32]{0,1:T(8,128)(2,1)S(1)}, bf16[1024,32]{0,1:T(8,128)(2,1)}, u32[]{:S(2)}) copy-start(bf16[1024,32]{0,1:T(8,128)(2,1)} %param.9) | copy-start | bytes 196612
  6.5 2.9 %copy-start.1 = (bf16[2,256,1024]{2,1,0:T(8,128)(2,1)S(1)}, bf16[2,256,1024]{2,1,0:T(8,128)(2,1)}, u32[]{:S(2)}) copy-start(bf16[2,256,1024]{2,1,0:T(8,128)(2,1)} %param.6) | copy-start | bytes 3145732
  6.5 67.7 %all-gather.3.cloned.1.call-start = ((), (), s32[]{:S(2)}) async-start(), calls=%async_computation.2 | async-start | bytes 6684672 | tf_op jit(solution)/shard_map/all_gather | solution.py:24
  7.3 109.7 %all-gather.5.cloned.1.call-start = ((), (), s32[]{:S(2)}) async-start(), calls=%async_computation.3 | async-start | bytes 2228224 | tf_op jit(solution)/shard_map/all_gather | solution.py:38
  108.8 6.3 %copy-start.2 = (bf16[2,256,1,16,64]{1,4,3,0,2:T(8,128)(2,1)S(1)}, bf16[2,256,1,16,64]{1,4,3,0,2:T(8,128)(2,1)}, u32[]{:S(2)}) copy-start(bf16[2,256,1,16,64]{1,4,3,0,2:T(8,128)(2,1)} %copy.47) | copy-start | bytes 3145732
  140.1 11.4 %all-to-all-start.1 = ((bf16[2,32,1024]{2,0,1:T(2,128)(2,1)}), bf16[2,32,1024]{2,0,1:T(2,128)(2,1)S(1)}, u32[]{:S(2)}, u32[]{:S(2)}) async-start(bf16[2,32,1024]{2,0,1:T(2,128)(2,1)} %bitcast.27), calls=%async_computation.1 | async-start | bytes 262144 | tf_op jit(solution)/shard_map/all_to_all | solution.py:66
Sparse Core Ops, SparseCore 0:
  9.6 64.5 all-gather.2
  76.4 39.9 all-gather.4
where the time goes:
time: 160 us
  waiting for transfers between devices  73.3 us (46%)
  local copies, waits for them, and re-layouts  25.1 us (16%)
  matrix products  24 us (15%)
  between operations  13.5 us (8%)
  blocking collectives  11.3 us (7%)
  other arithmetic  9.08 us (6%)
  starting transfers between devices  3.55 us (2%)
    all_gather x1, waiting for transfers between devices, on_device(): full_qkv = lax.all_gather(w_qkv, 'expert', axis=0, tiled=True)  64 us
    all_to_all x1, blocking collectives, on_device(): lax.all_to_all(slot_inputs, 'expert', split_axis=1, concat_axis=1, tiled=...  11.3 us
    unnamed x9, local copies, waits for them, and re-layouts  9.61 us
    reshape x1, local copies, waits for them, and re-layouts, on_device(): qkv.astype(jnp.bfloat16)  8.6 us
    all_to_all x1, waiting for transfers between devices, on_device(): lax.all_to_all(answered, 'expert', split_axis=1, concat_axis=1, tiled=True)  7.85 us
    dot_general x1, matrix products, on_device(): qkv = jnp.dot(normed, full_qkv, preferred_element_type=jnp.float32)  7.53 us
    sub x1, other arithmetic, on_device(): weights = jax.nn.softmax(scores, axis=-1).astype(jnp.bfloat16)  6.31 us
    dot_general x1, matrix products, on_device(): jnp.einsum('bneph,ehd->bnepd', hidden, w_expert_out, preferred_element_ty...  6.09 us
  transfers between devices with their start and end apart: 3, of which 2 were waited for; matrix products, arithmetic and copies ran while one was open for 28% of the time, Pallas kernels for 0%

commit v1 on v0

--- a/solution.py
+++ b/solution.py
@@ -5,6 +5,22 @@
 from jax.sharding import PartitionSpec as P
 
 HEADS = 16
+
+
+def pairwise_exchange(x, axis, split, join):
+    ways, here = (lax.axis_size(axis), lax.axis_index(axis))
+    width = x.shape[split] // ways
+    shape = list(x.shape)
+    shape[split] = width
+    height = shape[join]
+    shape[join] = height * ways
+    full = jnp.zeros(shape, x.dtype)
+    for mask in range(ways):
+        part = lax.dynamic_slice_in_dim(x, (here ^ mask) * width, width, axis=split)
+        if mask:
+            part = lax.ppermute(part, axis, [(d, d ^ mask) for d in range(ways)])
+        full = lax.dynamic_update_slice_in_dim(full, part, (here ^ mask) * height, axis=join)
+    return full
 
 
 def layer_norm(values):
@@ -52,7 +68,7 @@
     sources = lax.axis_size("expert")
     expert_here = w_expert_in.shape[0]
     pairs = slot_count // (sources * expert_here)
-    block = lax.all_to_all(slot_inputs, "expert", split_axis=1, concat_axis=1, tiled=True)
+    block = pairwise_exchange(slot_inputs, "expert", 1, 1)
     batch = block.shape[0]
     arranged = block.reshape(batch, sources, expert_here, pairs, model_width)
     hidden = jnp.einsum(

time: 160 us -> 175 us (1.094)
  starting transfers between devices: 3.55 us -> 25.3 us
  blocking collectives: 11.3 us -> 0 us
  waiting for transfers between devices: 73.3 us -> 76.5 us
    ppermute x0 -> x15, starting transfers between devices: none -> 21.1 us  [pairwise_exchange(): part = lax.ppermute(part, axis, [(d, d ^ mask) for d in range(ways)])]
    all_to_all x1 -> x0, blocking collectives: 11.3 us -> none  [on_device(): lax.all_to_all(slot_inputs, 'expert', split_axis=1, concat_axis=1, tiled=...]
    ppermute x0 -> x15, waiting for transfers between devices: none -> 3.36 us  [pairwise_exchange(): part = lax.ppermute(part, axis, [(d, d ^ mask) for d in range(ways)])]
  transfers between devices with their start and end apart: 3 -> 18, of which waited for: 2 -> 4; matrix products, arithmetic and copies ran while one was open for 28% -> 26% of each run, Pallas kernels for 0% -> 0%
where the time goes in v1:
time: 175 us; the launch traced here: 174 us
  waiting for transfers between devices  76.5 us (44%)
  local copies, waits for them, and re-layouts  25.5 us (15%)
  starting transfers between devices  25.3 us (14%)
  matrix products  24 us (14%)
  between operations  13.8 us (8%)
  other arithmetic  9.25 us (5%)
    all_gather x1, waiting for transfers between devices, on_device(): full_qkv = lax.all_gather(w_qkv, 'expert', axis=0, tiled=True)  63.9 us
    ppermute x15, starting transfers between devices, pairwise_exchange(): part = lax.ppermute(part, axis, [(d, d ^ mask) for d in range(ways)])  21.1 us
    unnamed x9, local copies, waits for them, and re-layouts  9.61 us
    reshape x1, local copies, waits for them, and re-layouts, on_device(): qkv.astype(jnp.bfloat16)  8.6 us
    all_to_all x1, waiting for transfers between devices, on_device(): lax.all_to_all(answered, 'expert', split_axis=1, concat_axis=1, tiled=True)  7.89 us
    dot_general x1, matrix products, on_device(): qkv = jnp.dot(normed, full_qkv, preferred_element_type=jnp.float32)  7.53 us
    sub x1, other arithmetic, on_device(): weights = jax.nn.softmax(scores, axis=-1).astype(jnp.bfloat16)  6.49 us
    dot_general x1, matrix products, on_device(): jnp.einsum('bneph,ehd->bnepd', hidden, w_expert_out, preferred_element_ty...  6.1 us
  transfers between devices with their start and end apart: 18, of which 4 were waited for; matrix products, arithmetic and copies ran while one was open for 26% of the time, Pallas kernels for 0%

profile of v1, /device:TPU:0, one launch (start us, length us, event | category | flops | bytes accessed | tf_op | source)
XLA Modules:
  0.0 174.4 jit_solution(3362363271507452567)
XLA Ops:
  6.5 0.7 all-gather.3.cloned.1.call-update
  7.3 0.7 all-gather.5.cloned.1.call-update
  8.1 1.4 convert_reduce_fusion
  10.4 63.9 %all-gather.3.cloned.1.call-done = bf16[1024,3072]{1,0:T(8,128)(2,1)} async-done(((bf16[64,3072]{1,0:T(8,128)(2,1)}), bf16[1024,3072]{1,0:T(8,128)(2,1)}) %all-gather.3.cloned.1.call-update) | async-done | bytes 6291472 | tf_op jit(solution)/shard_map/all_gather | solution.py:40
  74.2 7.5 %convolution_convert_fusion = bf16[512,3072]{1,0:T(8,128)(2,1)} fusion(bf16[512,1024]{1,0:T(8,128)(2,1)S(1)} %bitcast.133, bf16[1024,3072]{1,0:T(8,128)(2,1)} %all-gather.3.cloned.1.call-done), kind=kOutput, calls=%fused_computation.7 | convolution fusion | flops 3222798336 | bytes 10485760 | tf_op jit(solution)/shard_map/dot_general | solution.py:41
  81.8 8.6 %reshape.80 = bf16[2,256,3,16,64]{4,3,2,1,0:T(8,128)(2,1)} reshape(bf16[512,3072]{1,0:T(8,128)(2,1)} %convolution_convert_fusion) | data formatting | bytes 6291456 | tf_op jit(solution)/shard_map/reshape | solution.py:42
  90.4 6.0 %fusion.110 = (bf16[2,256,1,16,64]{4,3,2,1,0:T(8,128)(2,1)S(1)}, bf16[2,256,1,16,64]{4,3,2,1,0:T(8,128)(2,1)}, bf16[2,256,1,16,64]{4,3,2,1,0:T(8,128)(2,1)}) fusion(bf16[2,256,3,16,64]{4,3,2,1,0:T(8,128)(2,1)} %reshape.80), kind=kLoop, calls=%fused_computation.150 | loop fusion | bytes 6291456 | tf_op jit(solution)/shard_map/slice | solution.py:45
  96.4 3.6 %copy.69 = bf16[2,256,1,16,64]{1,4,3,0,2:T(8,128)(2,1)} copy(bf16[2,256,1,16,64]{4,3,2,1,0:T(8,128)(2,1)} %get-tuple-element.6) | data formatting | bytes 2097152
  99.9 3.5 %copy.70 = bf16[2,256,1,16,64]{1,4,3,0,2:T(8,128)(2,1)} copy(bf16[2,256,1,16,64]{4,3,2,1,0:T(8,128)(2,1)} %get-tuple-element.7) | data formatting | bytes 2097152
  103.5 2.5 %copy.68 = bf16[2,256,1,16,64]{1,4,3,0,2:T(8,128)(2,1)} copy(bf16[2,256,1,16,64]{4,3,2,1,0:T(8,128)(2,1)S(1)} %get-tuple-element.5) | data formatting | bytes 2097152
  106.0 2.8 %fusion.31 = f32[2,16,256,256]{2,3,1,0:T(8,128)S(1)} fusion(bf16[2,256,1,16,64]{1,4,3,0,2:T(8,128)(2,1)} %copy.70, bf16[2,256,1,16,64]{1,4,3,0,2:T(8,128)(2,1)} %copy.69), kind=kOutput, calls=%fused_computation.34 | convolution fusion | flops 268435456 | bytes 10485760 | tf_op jit(solution)/shard_map/bqhd,bkhd->bhqk/dot_general | solution.py:46
  108.8 6.5 %fusion.111 = (f32[2,16,256]{2,1,0:T(8,128)S(1)}, f32[2,16,256,256]{2,3,1,0:T(8,128)S(1)}) fusion(f32[2,16,256,256]{2,3,1,0:T(8,128)S(1)} %fusion.31), kind=kOutput, calls=%fused_computation.151 | output fusion | flops 8388863 | bytes 16809984 | tf_op jit(solution)/shard_map/sub | solution.py:49
  115.3 1.8 %fusion.20 = bf16[2,16,64,256]{3,2,1,0:T(8,128)(2,1)} fusion(f32[2,16,256,256]{2,3,1,0:T(8,128)S(1)} %get-tuple-element.25, f32[2,16,256]{2,1,0:T(8,128)S(1)} %get-tuple-element.24, bf16[2,256,1,16,64]{1,4,3,0,2:T(8,128)(2,1)S(1)} %copy-done.2), kind=kOutput, calls=%fused_computation.26 | convolution fusion | flops 273154048 | bytes 10518528 | tf_op jit(solution)/shard_map/bhqk,bkhd->bqhd/dot_general | solution.py:50
  117.1 3.3 %fusion.112 = (f32[2,256]{1,0:T(2,128)S(1)}, f32[2,256,1024]{2,1,0:T(8,128)S(1)}) fusion(bf16[2,256,1024]{1,2,0:T(8,128)(2,1)} %bitcast.134, bf16[1024,1024]{1,0:T(8,128)(2,1)} %all-gather.5.cloned.1.call-done, bf16[2,256,1024]{2,1,0:T(8,128)(2,1)S(1)} %copy-done.1), kind=kOutput, calls=%fused_computation.152 | convolution fusion | flops 1075314176 | bytes 6293504 | tf_op jit(solution)/shard_map/dot_general | solution.py:55
  123.1 1.0 collective-permute-start.2
  124.1 1.5 collective-permute-start.3
  126.1 1.5 collective-permute-start.5
  127.7 1.1 collective-permute-start.6
  128.8 2.2 %collective-permute-start.7 = (bf16[2,2,1024]{2,1,0:T(2,128)(2,1)S(1)}, bf16[2,2,1024]{2,1,0:T(2,128)(2,1)S(1)}, u32[]{:S(2)}, u32[]{:S(2)}) collective-permute-start(bf16[2,2,1024]{2,1,0:T(2,128)(2,1)S(1)} %get-tuple-element.15), channel_id=1, source_target_pairs={{0,8},{1,9},{2,10},{3,11},{4,12},{5,13},{6,14},{7,15},{8,0},{9,1},... | collective-permute-start | bytes 24584 | tf_op jit(solution)/shard_map/ppermute | solution.py:21
  131.8 2.0 %collective-permute-start.9 = (bf16[2,2,1024]{2,1,0:T(2,128)(2,1)S(1)}, bf16[2,2,1024]{2,1,0:T(2,128)(2,1)S(1)}, u32[]{:S(2)}, u32[]{:S(2)}) collective-permute-start(bf16[2,2,1024]{2,1,0:T(2,128)(2,1)S(1)} %get-tuple-element.13), channel_id=1, source_target_pairs={{0,10},{1,11},{2,8},{3,9},{4,14},{5,15},{6,12},{7,13},{8,2},{9,3},... | collective-permute-start | bytes 24584 | tf_op jit(solution)/shard_map/ppermute | solution.py:21
  133.8 1.5 collective-permute-start.10
  135.4 2.0 %collective-permute-start.11 = (bf16[2,2,1024]{2,1,0:T(2,128)(2,1)S(1)}, bf16[2,2,1024]{2,1,0:T(2,128)(2,1)S(1)}, u32[]{:S(2)}, u32[]{:S(2)}) collective-permute-start(bf16[2,2,1024]{2,1,0:T(2,128)(2,1)S(1)} %get-tuple-element.11), channel_id=1, source_target_pairs={{0,12},{1,13},{2,14},{3,15},{4,8},{5,9},{6,10},{7,11},{8,4},{9,5},... | collective-permute-start | bytes 24584 | tf_op jit(solution)/shard_map/ppermute | solution.py:21
  137.3 1.9 %collective-permute-start.12 = (bf16[2,2,1024]{2,1,0:T(2,128)(2,1)S(1)}, bf16[2,2,1024]{2,1,0:T(2,128)(2,1)S(1)}, u32[]{:S(2)}, u32[]{:S(2)}) collective-permute-start(bf16[2,2,1024]{2,1,0:T(2,128)(2,1)S(1)} %get-tuple-element.10), channel_id=1, source_target_pairs={{0,13},{1,12},{2,15},{3,14},{4,9},{5,8},{6,11},{7,10},{8,5},{9,4},... | collective-permute-start | bytes 24584 | tf_op jit(solution)/shard_map/ppermute | solution.py:21
  139.2 2.0 %collective-permute-start.13 = (bf16[2,2,1024]{2,1,0:T(2,128)(2,1)S(1)}, bf16[2,2,1024]{2,1,0:T(2,128)(2,1)S(1)}, u32[]{:S(2)}, u32[]{:S(2)}) collective-permute-start(bf16[2,2,1024]{2,1,0:T(2,128)(2,1)S(1)} %get-tuple-element.9), channel_id=1, source_target_pairs={{0,14},{1,15},{2,12},{3,13},{4,10},{5,11},{6,8},{7,9},{8,6},{9,7},... | collective-permute-start | bytes 24584 | tf_op jit(solution)/shard_map/ppermute | solution.py:21
  141.3 2.4 %collective-permute-start.14 = (bf16[2,2,1024]{2,1,0:T(2,128)(2,1)S(1)}, bf16[2,2,1024]{2,1,0:T(2,128)(2,1)S(1)}, u32[]{:S(2)}, u32[]{:S(2)}) collective-permute-start(bf16[2,2,1024]{2,1,0:T(2,128)(2,1)S(1)} %get-tuple-element.8), channel_id=1, source_target_pairs={{0,15},{1,14},{2,13},{3,12},{4,11},{5,10},{6,9},{7,8},{8,7},{9,6},... | collective-permute-start | bytes 24584 | tf_op jit(solution)/shard_map/ppermute | solution.py:21
  143.8 1.8 %collective-permute-done.13 = bf16[2,2,1024]{2,1,0:T(2,128)(2,1)S(1)} collective-permute-done((bf16[2,2,1024]{2,1,0:T(2,128)(2,1)S(1)}, bf16[2,2,1024]{2,1,0:T(2,128)(2,1)S(1)}, u32[]{:S(2)}, u32[]{:S(2)}) %collective-permute-start.13) | collective-permute-done | bytes 8224 | tf_op jit(solution)/shard_map/ppermute | solution.py:21
  145.7 1.5 collective-permute-done.14
  147.2 6.1 %fusion.24 = bf16[2,16,1,2,1024]{4,1,3,0,2:T(8,128)(2,1)S(1)} fusion(bf16[1,2048,1024]{2,1,0:T(8,128)(2,1)} %param.11, bf16[1,1024,2048]{2,1,0:T(8,128)(2,1)} %param.10, bf16[2,16,2,1024]{3,0,2,1:T(2,128)(2,1)S(1)} %bitcast.135), kind=kOutput, calls=%fused_computation.29 | convolution fusion | flops 545456128 | bytes 8650752 | tf_op jit(solution)/shard_map/bneph,ehd->bnepd/dot_general | solution.py:78
  153.3 0.8 copy.60
  154.1 4.1 %all-to-all-start = ((bf16[2,32,1024]{2,0,1:T(2,128)(2,1)}), bf16[2,32,1024]{2,0,1:T(2,128)(2,1)S(1)}, u32[]{:S(2)}, u32[]{:S(2)}) async-start(bf16[2,32,1024]{2,0,1:T(2,128)(2,1)} %bitcast.27), calls=%async_computation | async-start | bytes 262144 | tf_op jit(solution)/shard_map/all_to_all | solution.py:82
  158.2 7.9 %all-to-all-done = bf16[2,32,1024]{2,0,1:T(2,128)(2,1)S(1)} async-done(((bf16[2,32,1024]{2,0,1:T(2,128)(2,1)}), bf16[2,32,1024]{2,0,1:T(2,128)(2,1)S(1)}, u32[]{:S(2)}, u32[]{:S(2)}) %all-to-all-start) | async-done | bytes 131104 | tf_op jit(solution)/shard_map/all_to_all | solution.py:82
  166.1 1.5 add_convert_fusion
  (55 shorter events, 5.0 us)
Async XLA Ops:
  6.5 114.3 %copy-start = (bf16[1024,32]{0,1:T(8,128)(2,1)S(1)}, bf16[1024,32]{0,1:T(8,128)(2,1)}, u32[]{:S(2)}) copy-start(bf16[1024,32]{0,1:T(8,128)(2,1)} %param.9) | copy-start | bytes 196612
  6.5 3.0 %copy-start.1 = (bf16[2,256,1024]{2,1,0:T(8,128)(2,1)S(1)}, bf16[2,256,1024]{2,1,0:T(8,128)(2,1)}, u32[]{:S(2)}) copy-start(bf16[2,256,1024]{2,1,0:T(8,128)(2,1)} %param.6) | copy-start | bytes 3145732
  6.5 67.7 %all-gather.3.cloned.1.call-start = ((), (), s32[]{:S(2)}) async-start(), calls=%async_computation.1 | async-start | bytes 6684672 | tf_op jit(solution)/shard_map/all_gather | solution.py:40
  7.3 109.9 %all-gather.5.cloned.1.call-start = ((), (), s32[]{:S(2)}) async-start(), calls=%async_computation.2 | async-start | bytes 2228224 | tf_op jit(solution)/shard_map/all_gather | solution.py:54
  108.8 6.5 %copy-start.2 = (bf16[2,256,1,16,64]{1,4,3,0,2:T(8,128)(2,1)S(1)}, bf16[2,256,1,16,64]{1,4,3,0,2:T(8,128)(2,1)}, u32[]{:S(2)}) copy-start(bf16[2,256,1,16,64]{1,4,3,0,2:T(8,128)(2,1)} %copy.68) | copy-start | bytes 3145732
  122.2 3.9 %collective-permute-start = (bf16[2,2,1024]{2,1,0:T(2,128)(2,1)S(1)}, bf16[2,2,1024]{2,1,0:T(2,128)(2,1)S(1)}, u32[]{:S(2)}, u32[]{:S(2)}) collective-permute-start(bf16[2,2,1024]{2,1,0:T(2,128)(2,1)S(1)} %get-tuple-element.22), channel_id=1, source_target_pairs={{0,1},{1,0},{2,3},{3,2},{4,5},{5,4},{6,7},{7,6},{8,9},{9,8},{10,11... | collective-permute-start | bytes 24584 | tf_op jit(solution)/shard_map/ppermute | solution.py:21
  122.5 5.2 %collective-permute-start.1 = (bf16[2,2,1024]{2,1,0:T(2,128)(2,1)S(1)}, bf16[2,2,1024]{2,1,0:T(2,128)(2,1)S(1)}, u32[]{:S(2)}, u32[]{:S(2)}) collective-permute-start(bf16[2,2,1024]{2,1,0:T(2,128)(2,1)S(1)} %get-tuple-element.21), channel_id=1, source_target_pairs={{0,2},{1,3},{2,0},{3,1},{4,6},{5,7},{6,4},{7,5},{8,10},{9,11},{10,... | collective-permute-start | bytes 24584 | tf_op jit(solution)/shard_map/ppermute | solution.py:21
  123.1 5.7 %collective-permute-start.2 = (bf16[2,2,1024]{2,1,0:T(2,128)(2,1)S(1)}, bf16[2,2,1024]{2,1,0:T(2,128)(2,1)S(1)}, u32[]{:S(2)}, u32[]{:S(2)}) collective-permute-start(bf16[2,2,1024]{2,1,0:T(2,128)(2,1)S(1)} %get-tuple-element.20), channel_id=1, source_target_pairs={{0,3},{1,2},{2,1},{3,0},{4,7},{5,6},{6,5},{7,4},{8,11},{9,10},{10,... | collective-permute-start | bytes 24584 | tf_op jit(solution)/shard_map/ppermute | solution.py:21
  124.1 6.9 %collective-permute-start.3 = (bf16[2,2,1024]{2,1,0:T(2,128)(2,1)S(1)}, bf16[2,2,1024]{2,1,0:T(2,128)(2,1)S(1)}, u32[]{:S(2)}, u32[]{:S(2)}) collective-permute-start(bf16[2,2,1024]{2,1,0:T(2,128)(2,1)S(1)} %get-tuple-element.19), channel_id=1, source_target_pairs={{0,4},{1,5},{2,6},{3,7},{4,0},{5,1},{6,2},{7,3},{8,12},{9,13},{10,... | collective-permute-start | bytes 24584 | tf_op jit(solution)/shard_map/ppermute | solution.py:21
  125.6 6.2 %collective-permute-start.4 = (bf16[2,2,1024]{2,1,0:T(2,128)(2,1)S(1)}, bf16[2,2,1024]{2,1,0:T(2,128)(2,1)S(1)}, u32[]{:S(2)}, u32[]{:S(2)}) collective-permute-start(bf16[2,2,1024]{2,1,0:T(2,128)(2,1)S(1)} %get-tuple-element.18), channel_id=1, source_target_pairs={{0,5},{1,4},{2,7},{3,6},{4,1},{5,0},{6,3},{7,2},{8,13},{9,12},{10,... | collective-permute-start | bytes 24584 | tf_op jit(solution)/shard_map/ppermute | solution.py:21
  126.1 7.7 %collective-permute-start.5 = (bf16[2,2,1024]{2,1,0:T(2,128)(2,1)S(1)}, bf16[2,2,1024]{2,1,0:T(2,128)(2,1)S(1)}, u32[]{:S(2)}, u32[]{:S(2)}) collective-permute-start(bf16[2,2,1024]{2,1,0:T(2,128)(2,1)S(1)} %get-tuple-element.17), channel_id=1, source_target_pairs={{0,6},{1,7},{2,4},{3,5},{4,2},{5,3},{6,0},{7,1},{8,14},{9,15},{10,... | collective-permute-start | bytes 24584 | tf_op jit(solution)/shard_map/ppermute | solution.py:21
  127.7 7.7 %collective-permute-start.6 = (bf16[2,2,1024]{2,1,0:T(2,128)(2,1)S(1)}, bf16[2,2,1024]{2,1,0:T(2,128)(2,1)S(1)}, u32[]{:S(2)}, u32[]{:S(2)}) collective-permute-start(bf16[2,2,1024]{2,1,0:T(2,128)(2,1)S(1)} %get-tuple-element.16), channel_id=1, source_target_pairs={{0,7},{1,6},{2,5},{3,4},{4,3},{5,2},{6,1},{7,0},{8,15},{9,14},{10,... | collective-permute-start | bytes 24584 | tf_op jit(solution)/shard_map/ppermute | solution.py:21
  128.8 8.5 %collective-permute-start.7 = (bf16[2,2,1024]{2,1,0:T(2,128)(2,1)S(1)}, bf16[2,2,1024]{2,1,0:T(2,128)(2,1)S(1)}, u32[]{:S(2)}, u32[]{:S(2)}) collective-permute-start(bf16[2,2,1024]{2,1,0:T(2,128)(2,1)S(1)} %get-tuple-element.15), channel_id=1, source_target_pairs={{0,8},{1,9},{2,10},{3,11},{4,12},{5,13},{6,14},{7,15},{8,0},{9,1},... | collective-permute-start | bytes 24584 | tf_op jit(solution)/shard_map/ppermute | solution.py:21
  131.1 8.1 %collective-permute-start.8 = (bf16[2,2,1024]{2,1,0:T(2,128)(2,1)S(1)}, bf16[2,2,1024]{2,1,0:T(2,128)(2,1)S(1)}, u32[]{:S(2)}, u32[]{:S(2)}) collective-permute-start(bf16[2,2,1024]{2,1,0:T(2,128)(2,1)S(1)} %get-tuple-element.14), channel_id=1, source_target_pairs={{0,9},{1,8},{2,11},{3,10},{4,13},{5,12},{6,15},{7,14},{8,1},{9,0},... | collective-permute-start | bytes 24584 | tf_op jit(solution)/shard_map/ppermute | solution.py:21
  131.8 9.5 %collective-permute-start.9 = (bf16[2,2,1024]{2,1,0:T(2,128)(2,1)S(1)}, bf16[2,2,1024]{2,1,0:T(2,128)(2,1)S(1)}, u32[]{:S(2)}, u32[]{:S(2)}) collective-permute-start(bf16[2,2,1024]{2,1,0:T(2,128)(2,1)S(1)} %get-tuple-element.13), channel_id=1, source_target_pairs={{0,10},{1,11},{2,8},{3,9},{4,14},{5,15},{6,12},{7,13},{8,2},{9,3},... | collective-permute-start | bytes 24584 | tf_op jit(solution)/shard_map/ppermute | solution.py:21
  133.8 9.9 %collective-permute-start.10 = (bf16[2,2,1024]{2,1,0:T(2,128)(2,1)S(1)}, bf16[2,2,1024]{2,1,0:T(2,128)(2,1)S(1)}, u32[]{:S(2)}, u32[]{:S(2)}) collective-permute-start(bf16[2,2,1024]{2,1,0:T(2,128)(2,1)S(1)} %get-tuple-element.12), channel_id=1, source_target_pairs={{0,11},{1,10},{2,9},{3,8},{4,15},{5,14},{6,13},{7,12},{8,3},{9,2},... | collective-permute-start | bytes 24584 | tf_op jit(solution)/shard_map/ppermute | solution.py:21
  135.4 8.4 %collective-permute-start.11 = (bf16[2,2,1024]{2,1,0:T(2,128)(2,1)S(1)}, bf16[2,2,1024]{2,1,0:T(2,128)(2,1)S(1)}, u32[]{:S(2)}, u32[]{:S(2)}) collective-permute-start(bf16[2,2,1024]{2,1,0:T(2,128)(2,1)S(1)} %get-tuple-element.11), channel_id=1, source_target_pairs={{0,12},{1,13},{2,14},{3,15},{4,8},{5,9},{6,10},{7,11},{8,4},{9,5},... | collective-permute-start | bytes 24584 | tf_op jit(solution)/shard_map/ppermute | solution.py:21
  137.3 6.4 %collective-permute-start.12 = (bf16[2,2,1024]{2,1,0:T(2,128)(2,1)S(1)}, bf16[2,2,1024]{2,1,0:T(2,128)(2,1)S(1)}, u32[]{:S(2)}, u32[]{:S(2)}) collective-permute-start(bf16[2,2,1024]{2,1,0:T(2,128)(2,1)S(1)} %get-tuple-element.10), channel_id=1, source_target_pairs={{0,13},{1,12},{2,15},{3,14},{4,9},{5,8},{6,11},{7,10},{8,5},{9,4},... | collective-permute-start | bytes 24584 | tf_op jit(solution)/shard_map/ppermute | solution.py:21
  139.2 6.4 %collective-permute-start.13 = (bf16[2,2,1024]{2,1,0:T(2,128)(2,1)S(1)}, bf16[2,2,1024]{2,1,0:T(2,128)(2,1)S(1)}, u32[]{:S(2)}, u32[]{:S(2)}) collective-permute-start(bf16[2,2,1024]{2,1,0:T(2,128)(2,1)S(1)} %get-tuple-element.9), channel_id=1, source_target_pairs={{0,14},{1,15},{2,12},{3,13},{4,10},{5,11},{6,8},{7,9},{8,6},{9,7},... | collective-permute-start | bytes 24584 | tf_op jit(solution)/shard_map/ppermute | solution.py:21
  141.3 5.8 %collective-permute-start.14 = (bf16[2,2,1024]{2,1,0:T(2,128)(2,1)S(1)}, bf16[2,2,1024]{2,1,0:T(2,128)(2,1)S(1)}, u32[]{:S(2)}, u32[]{:S(2)}) collective-permute-start(bf16[2,2,1024]{2,1,0:T(2,128)(2,1)S(1)} %get-tuple-element.8), channel_id=1, source_target_pairs={{0,15},{1,14},{2,13},{3,12},{4,11},{5,10},{6,9},{7,8},{8,7},{9,6},... | collective-permute-start | bytes 24584 | tf_op jit(solution)/shard_map/ppermute | solution.py:21
  154.1 12.1 %all-to-all-start = ((bf16[2,32,1024]{2,0,1:T(2,128)(2,1)}), bf16[2,32,1024]{2,0,1:T(2,128)(2,1)S(1)}, u32[]{:S(2)}, u32[]{:S(2)}) async-start(bf16[2,32,1024]{2,0,1:T(2,128)(2,1)} %bitcast.27), calls=%async_computation | async-start | bytes 262144 | tf_op jit(solution)/shard_map/all_to_all | solution.py:82
Sparse Core Ops, SparseCore 0:
  9.6 64.5 all-gather.2
  76.4 39.9 all-gather.4
